TPU v7x, 256 devices: a whole 4x4x8 slice. The times are simulated.
256 devices in a mesh: sub: 128 (over x, y, z_hi, core), panel: 2 (over z_lo).
Axes of the slice: x: 4, y: 4, z: 8 (z_hi: 4, z_lo: 2; z = z_hi * 2 + z_lo), core: 2. Of those that a mesh axis runs over, the one named last changes fastest.
Arguments:
- solution: float32 [131072, 256], P('sub', 'panel'), may hold values from -6 to 6
- residual: float32 [131072, 256], P('sub', 'panel'), may hold values from -25 to 25
- shadow: float32 [131072, 256], P('sub', 'panel'), may hold values from -120 to 120
- direction: float32 [131072, 256], P('sub', 'panel'), may hold values from -6 to 6
- old_image: float32 [131072, 256], P('sub', 'panel'), may hold values from -6 to 6
- rho_prev: float32 [256], P('panel'), may hold values from 1 to 4
- alpha_prev: float32 [256], P('panel'), may hold values from 0.5 to 2
- omega_prev: float32 [256], P('panel'), may hold values from 0.5 to 2
- lower_inverse: bfloat16 [128, 1792, 1792], P('sub', None, 'panel'), may hold values from -0.4 to 0.4, as said below
- upper_inverse: bfloat16 [128, 1792, 1792], P('sub', None, 'panel'), may hold values from -0.4 to 0.4, as said below
- neighbours: int32 [16, 131072], P(None, 'sub'), may hold values from 0 to 1792, as said below
- edge_weight: float32 [16, 131072], P(None, 'sub'), may hold values from 0.1 to 1
- node_shift: float32 [131072], P('sub'), may hold values from 3 to 12
- send_rows: int32 [128, 2, 384], P('sub'), may hold values from 0 to 1023
Outputs:
- new_solution: float32 [131072, 256], P('sub', 'panel')
- new_residual: float32 [131072, 256], P('sub', 'panel')
- step_alpha: float32 [256], P('panel')
- step_omega: float32 [256], P('panel')
- next_rho: float32 [256], P('panel')
Inputs may be any that keep to these rules, and one draw needn't show every extreme that they name: lower_inverse[s] is zero above its diagonal. upper_inverse[s] is zero below its diagonal. `neighbours`: an entry below 1024 is an owned node, from 1024 a ghost node from the lower neighbour's list, from 1408 one from the upper neighbour's list; 1792 marks an empty slot. send_rows[s, 0] lists the rows of subdomain s that subdomain s - 1 holds as ghosts, send_rows[s, 1] those that subdomain s + 1 holds, modulo 128.
All inputs are finite; a program needn't handle non-finite values.
Results may differ from a plain program's by a relative error of at most 0.0097.
Values may be sent and summed in bfloat16 or wider, within the bound.
A program may use at most 64 MiB of HBM per device.

v0:
```python
import functools
import jax
import jax.numpy as jnp
from jax import lax
from jax.sharding import Mesh
from jax.sharding import PartitionSpec as P

SUB = ("sub_0", "sub_1", "sub_2", "sub_3")
FLOOR_SHARE = 0.3
EPSILON = 1e-06


def padded_2(cells, sides, width):
    for axis, dim in sides:
        count = lax.axis_size(axis)
        head = lax.slice_in_dim(cells, 0, width, axis=dim)
        tail = lax.slice_in_dim(cells, cells.shape[dim] - width, cells.shape[dim], axis=dim)
        cells = jnp.concatenate(
            [
                lax.ppermute(tail, axis, [(i, (i + 1) % count) for i in range(count)]),
                cells,
                lax.ppermute(head, axis, [((i + 1) % count, i) for i in range(count)]),
            ],
            axis=dim,
        )
    return cells


def in_blocks(array, dim, devices):
    lengths = array.shape
    blocks = array.reshape(*lengths[:dim], devices, lengths[dim] // devices, *lengths[dim + 1 :])
    return jnp.moveaxis(blocks, dim, 0)


def sent_and_summed(array, axis, dim):
    devices = lax.axis_size(axis)
    blocks = lax.all_to_all(in_blocks(array, dim, devices), axis, 0, 0, tiled=True)
    return jnp.sum(blocks, axis=0)


def one_axis_at_a_time(array, axes):
    return functools.reduce(lax.psum, axes, array)


def extend(vector, send_rows):
    outgoing = jnp.concatenate([vector[send_rows[0, 0]], vector[send_rows[0, 1]]], axis=0)
    border = send_rows.shape[2]
    padded = padded_2(outgoing, ((SUB, 0),), border)
    return jnp.concatenate([vector, padded[:border], padded[3 * border :]], axis=0)


def operate(vector, send_rows, neighbours, edge_weight, node_shift):
    extended = extend(vector, send_rows)
    ext_rows = extended.shape[0]
    padded = jnp.concatenate([extended, jnp.zeros((1, vector.shape[1]), jnp.float32)], axis=0)
    present = jnp.where(neighbours < ext_rows, edge_weight, 0.0)
    coupled = jnp.sum(present[:, :, None] * padded[neighbours], axis=0)
    diagonal = node_shift + jnp.sum(present, axis=0)
    return diagonal[:, None] * vector - coupled


def precondition(vector, send_rows, factors):
    lower_panel, upper_panel = factors
    own_rows, local_sources = vector.shape
    rounded = extend(vector, send_rows).astype(jnp.bfloat16)
    columns = lax.all_to_all(rounded, "panel", split_axis=0, concat_axis=1, tiled=True)
    inner_part = sent_and_summed(
        jnp.dot(lower_panel, columns, preferred_element_type=jnp.float32), "panel", 0
    ).astype(jnp.bfloat16)
    partial_sum = jnp.dot(upper_panel[:own_rows], inner_part, preferred_element_type=jnp.float32)
    return sent_and_summed(partial_sum, "panel", 1)


def per_device(
    solution,
    residual,
    shadow,
    direction,
    old_image,
    rho_prev,
    alpha_prev,
    omega_prev,
    lower_inverse,
    upper_inverse,
    neighbours,
    edge_weight,
    node_shift,
    send_rows,
):
    node_count = residual.shape[0] * lax.axis_size(SUB)
    factors = (lower_inverse[0], upper_inverse[0])
    opening = (
        one_axis_at_a_time(jnp.sum(shadow * residual, axis=0), SUB),
        one_axis_at_a_time(jnp.sum(shadow * shadow, axis=0), SUB),
    )
    rho_now = opening[0] / node_count
    shadow_square = opening[1] / node_count
    step_beta = rho_now / rho_prev * (alpha_prev / omega_prev)
    new_direction = residual + step_beta * (direction - omega_prev * old_image)
    direction_hat = precondition(new_direction, send_rows, factors)
    image_new = operate(direction_hat, send_rows, neighbours, edge_weight, node_shift)
    second = (
        one_axis_at_a_time(jnp.sum(shadow * image_new, axis=0), SUB),
        one_axis_at_a_time(jnp.sum(image_new * image_new, axis=0), SUB),
    )
    denominator = second[0] / node_count
    image_square = second[1] / node_count
    step_alpha = rho_now / jnp.maximum(
        denominator, FLOOR_SHARE * jnp.sqrt(shadow_square * image_square)
    )
    middle = residual - step_alpha * image_new
    middle_hat = precondition(middle, send_rows, factors)
    tested = operate(middle_hat, send_rows, neighbours, edge_weight, node_shift)
    closing = (
        one_axis_at_a_time(jnp.sum(tested * middle, axis=0), SUB),
        one_axis_at_a_time(jnp.sum(tested * tested, axis=0), SUB),
        one_axis_at_a_time(jnp.sum(shadow * middle, axis=0), SUB),
        one_axis_at_a_time(jnp.sum(shadow * tested, axis=0), SUB),
    )
    step_omega = closing[0] / node_count / (closing[1] / node_count + EPSILON)
    new_residual = middle - step_omega * tested
    next_rho = closing[2] / node_count - step_omega * (closing[3] / node_count)
    new_solution = solution + step_alpha * direction_hat + step_omega * middle_hat
    return (new_solution, new_residual, step_alpha, step_omega, next_rho)


def solution(mesh):
    torus = Mesh(
        mesh.devices.reshape(4, 4, 4, 2, mesh.shape["panel"]),
        ("sub_0", "sub_1", "sub_2", "sub_3", "panel"),
    )
    in_specs = (
        P(SUB, "panel"),
        P(SUB, "panel"),
        P(SUB, "panel"),
        P(SUB, "panel"),
        P(SUB, "panel"),
        P("panel"),
        P("panel"),
        P("panel"),
        P(SUB, None, "panel"),
        P(SUB, None, "panel"),
        P(None, SUB),
        P(None, SUB),
        P(SUB),
        P(SUB, None, None),
    )
    out_specs = (P(SUB, "panel"), P(SUB, "panel"), P("panel"), P("panel"), P("panel"))
    return jax.shard_map(
        per_device, mesh=torus, in_specs=in_specs, out_specs=out_specs, check_vma=False
    )
```

profile of v0, /device:TPU:1, one launch (start us, length us, event | category | flops | bytes accessed | tf_op | source)
XLA Modules:
  0.0 427.7 jit_solution(668824493730074484)
XLA Ops:
  2.1 9.3 %psum.224 = f32[128]{0:T(128)S(1)} all-reduce(f32[128]{0:T(128)S(1)} %multiply_reduce_fusion.9), channel_id=1, replica_groups=mesh['sub_0'=4,'sub_1'=4,'sub_2'=4,'sub_3'=2,'panel'=2] {'sub_0'}, use_global_device_ids=true, to_apply=%region_1.0 | all-reduce | flops 128 | bytes 1024 | tf_op jit(solution)/shard_map/psum | solution.py:42
  11.4 9.0 %psum.225 = f32[128]{0:T(128)S(1)} all-reduce(f32[128]{0:T(128)S(1)} %psum.224), channel_id=1, replica_groups=mesh['sub_0'=4,'sub_1'=4,'sub_2'=4,'sub_3'=2,'panel'=2] {'sub_1'}, use_global_device_ids=true, to_apply=%region_2.0 | all-reduce | flops 128 | bytes 1024 | tf_op jit(solution)/shard_map/psum | solution.py:42
  20.4 12.9 %psum.226 = f32[128]{0:T(128)S(1)} all-reduce(f32[128]{0:T(128)S(1)} %psum.225), channel_id=1, replica_groups=mesh['sub_0'=4,'sub_1'=4,'sub_2'=4,'sub_3'=2,'panel'=2] {'sub_2'}, use_global_device_ids=true, to_apply=%region_3.0 | all-reduce | flops 128 | bytes 1024 | tf_op jit(solution)/shard_map/psum | solution.py:42
  33.3 8.6 %psum.227 = f32[128]{0:T(128)S(1)} all-reduce(f32[128]{0:T(128)S(1)} %psum.226), channel_id=1, replica_groups=mesh['sub_0'=4,'sub_1'=4,'sub_2'=4,'sub_3'=2,'panel'=2] {'sub_3'}, use_global_device_ids=true, to_apply=%region_4.0 | all-reduce | flops 128 | bytes 1024 | tf_op jit(solution)/shard_map/psum | solution.py:42
  49.2 6.3 %collective-permute-done.1 = bf16[384,128]{1,0:T(8,128)(2,1)S(1)} collective-permute-done((bf16[384,128]{1,0:T(8,128)(2,1)}, bf16[384,128]{1,0:T(8,128)(2,1)S(1)}, u32[]{:S(2)}, u32[]{:S(2)}) %collective-permute-start.1) | collective-permute-done | bytes 98336 | tf_op jit(solution)/shard_map/ppermute | solution.py:22
  59.1 8.5 %all_to_all.52 = bf16[2,896,128]{1,2,0:T(8,128)(2,1)S(1)} all-to-all(bf16[2,896,128]{1,2,0:T(8,128)(2,1)} %copy.21), channel_id=1, replica_groups=mesh['sub_0'=4,'sub_1'=4,'sub_2'=4,'sub_3'=2,'panel'=2] {'panel'}, dimensions={0} | all-to-all | bytes 917504 | tf_op jit(solution)/shard_map/all_to_all | solution.py:66
  69.0 19.2 %all_to_all.53 = f32[2,896,256]{1,2,0:T(8,128)} all-to-all(f32[2,896,256]{1,2,0:T(8,128)S(1)} %bitcast.54), channel_id=1, replica_groups=mesh['sub_0'=4,'sub_1'=4,'sub_2'=4,'sub_3'=2,'panel'=2] {'panel'}, dimensions={0} | all-to-all | bytes 3670016 | tf_op jit(solution)/shard_map/all_to_all | solution.py:37
  90.7 3.5 fusion.6
  94.1 4.4 %all-to-all-start.2 = ((f32[2,1024,128]{1,2,0:T(8,128)}), f32[2,1024,128]{1,2,0:T(8,128)}, u32[]{:S(2)}, u32[]{:S(2)}) async-start(f32[2,1024,128]{1,2,0:T(8,128)} %bitcast.62), calls=%async_computation.2 | async-start | bytes 2097152 | tf_op jit(solution)/shard_map/all_to_all | solution.py:37
  98.6 8.2 %all-to-all-done.2 = f32[2,1024,128]{1,2,0:T(8,128)} async-done(((f32[2,1024,128]{1,2,0:T(8,128)}), f32[2,1024,128]{1,2,0:T(8,128)}, u32[]{:S(2)}, u32[]{:S(2)}) %all-to-all-start.2) | async-done | bytes 1048608 | tf_op jit(solution)/shard_map/all_to_all | solution.py:37
  116.3 12.4 %collective-permute-start.2 = (f32[384,128]{1,0:T(8,128)}, f32[384,128]{1,0:T(8,128)S(1)}, u32[]{:S(2)}, u32[]{:S(2)}) collective-permute-start(f32[384,128]{1,0:T(8,128)} %gather_fusion.2), channel_id=1, source_target_pairs={{0,2},{2,4},{4,6},{6,8},{8,10},{10,12},{12,14},{14,16},{16,18},{18... | collective-permute-start | bytes 589832 | tf_op jit(solution)/shard_map/ppermute | solution.py:20
  128.8 4.8 %collective-permute-done.2 = f32[384,128]{1,0:T(8,128)S(1)} collective-permute-done((f32[384,128]{1,0:T(8,128)}, f32[384,128]{1,0:T(8,128)S(1)}, u32[]{:S(2)}, u32[]{:S(2)}) %collective-permute-start.2) | collective-permute-done | bytes 196640 | tf_op jit(solution)/shard_map/ppermute | solution.py:20
  138.7 55.6 %gather_fusion.4 = f32[16384,128]{1,0:T(8,128)} fusion(f32[1793,128]{1,0:T(8,128)} %maximum_maximum_fusion, s32[16384]{0:T(1024)S(1)} %broadcast_clamp_fusion), kind=kCustom, calls=%fused_computation.4 | custom fusion | bytes 16842752 | tf_op jit(solution)/shard_map/gather | solution.py:57
  194.3 5.3 %multiply_reduce_fusion.1 = f32[1024,128]{1,0:T(8,128)S(1)} fusion(f32[16,1024,128]{2,1,0:T(8,128)} %bitcast.53, f32[16,1024]{1,0:T(8,128)S(1)} %get-tuple-element.49), kind=kLoop, calls=%fused_computation.11 | loop fusion | flops 4063232 | bytes 8978432 | tf_op jit(solution)/shard_map/reduce_sum | solution.py:57
  200.6 6.2 %all-reduce.5 = (f32[128]{0:T(128)S(1)}, f32[128]{0:T(128)S(1)}, f32[128]{0:T(128)S(1)}) all-reduce(f32[128]{0:T(128)S(1)} %get-tuple-element.10, f32[128]{0:T(128)S(1)} %get-tuple-element.11, f32[128]{0:T(128)S(1)} %get-tuple-element.9), channel_id=1, replica_groups=mesh['sub_0'=4,'sub_1'=4,'sub_2'=4,'sub_3'=2,'panel'=2] {'sub_0'}, use_global_device_ids=true, to_apply=%region_20.21 | all-reduce | flops 384 | bytes 3072 | tf_op jit(solution)/shard_map/psum | solution.py:42
  206.8 6.0 %all-reduce.3 = (f32[128]{0:T(128)S(1)}, f32[128]{0:T(128)S(1)}, f32[128]{0:T(128)S(1)}) all-reduce(f32[128]{0:T(128)S(1)} %get-tuple-element.32, f32[128]{0:T(128)S(1)} %get-tuple-element.33, f32[128]{0:T(128)S(1)} %get-tuple-element.34), channel_id=1, replica_groups=mesh['sub_0'=4,'sub_1'=4,'sub_2'=4,'sub_3'=2,'panel'=2] {'sub_1'}, use_global_device_ids=true, to_apply=%region_21.22 | all-reduce | flops 384 | bytes 3072 | tf_op jit(solution)/shard_map/psum | solution.py:42
  212.8 16.5 %all-reduce.1 = (f32[128]{0:T(128)S(1)}, f32[128]{0:T(128)S(1)}, f32[128]{0:T(128)S(1)}) all-reduce(f32[128]{0:T(128)S(1)} %get-tuple-element.25, f32[128]{0:T(128)S(1)} %get-tuple-element.26, f32[128]{0:T(128)S(1)} %get-tuple-element.27), channel_id=1, replica_groups=mesh['sub_0'=4,'sub_1'=4,'sub_2'=4,'sub_3'=2,'panel'=2] {'sub_2'}, use_global_device_ids=true, to_apply=%region_22.23 | all-reduce | flops 384 | bytes 3072 | tf_op jit(solution)/shard_map/psum | solution.py:42
  234.3 2.8 gather_fusion.6
  243.2 4.0 collective-permute-done.5
  250.0 8.5 %all_to_all.54 = bf16[2,896,128]{1,2,0:T(8,128)(2,1)S(1)} all-to-all(bf16[2,896,128]{1,2,0:T(8,128)(2,1)} %copy.29), channel_id=1, replica_groups=mesh['sub_0'=4,'sub_1'=4,'sub_2'=4,'sub_3'=2,'panel'=2] {'panel'}, dimensions={0} | all-to-all | bytes 917504 | tf_op jit(solution)/shard_map/all_to_all | solution.py:66
  259.8 19.9 %all_to_all.55 = f32[2,896,256]{1,2,0:T(8,128)} all-to-all(f32[2,896,256]{1,2,0:T(8,128)S(1)} %bitcast.55), channel_id=1, replica_groups=mesh['sub_0'=4,'sub_1'=4,'sub_2'=4,'sub_3'=2,'panel'=2] {'panel'}, dimensions={0} | all-to-all | bytes 3670016 | tf_op jit(solution)/shard_map/all_to_all | solution.py:37
  284.7 11.5 %all_to_all.56 = f32[2,1024,128]{1,2,0:T(8,128)} all-to-all(f32[2,1024,128]{1,2,0:T(8,128)S(1)} %bitcast.63), channel_id=1, replica_groups=mesh['sub_0'=4,'sub_1'=4,'sub_2'=4,'sub_3'=2,'panel'=2] {'panel'}, dimensions={0} | all-to-all | bytes 2097152 | tf_op jit(solution)/shard_map/all_to_all | solution.py:37
  305.7 14.1 %collective-permute-start.6 = (f32[384,128]{1,0:T(8,128)}, f32[384,128]{1,0:T(8,128)S(1)}, u32[]{:S(2)}, u32[]{:S(2)}) collective-permute-start(f32[384,128]{1,0:T(8,128)} %gather_fusion.7), channel_id=1, source_target_pairs={{0,2},{2,4},{4,6},{6,8},{8,10},{10,12},{12,14},{14,16},{16,18},{18... | collective-permute-start | bytes 589832 | tf_op jit(solution)/shard_map/ppermute | solution.py:20
  319.8 3.0 collective-permute-done.6
  322.8 5.1 %collective-permute-done.7 = f32[384,128]{1,0:T(8,128)S(1)} collective-permute-done((f32[384,128]{1,0:T(8,128)}, f32[384,128]{1,0:T(8,128)S(1)}, u32[]{:S(2)}, u32[]{:S(2)}) %collective-permute-start.7) | collective-permute-done | bytes 196640 | tf_op jit(solution)/shard_map/ppermute | solution.py:22
  330.2 55.6 %gather_fusion.9 = f32[16384,128]{1,0:T(8,128)} fusion(f32[1793,128]{1,0:T(8,128)} %maximum_maximum_fusion.1, s32[16384]{0:T(1024)S(1)} %copy-done.7), kind=kCustom, calls=%fused_computation.9 | custom fusion | bytes 16842752 | tf_op jit(solution)/shard_map/gather | solution.py:57
  385.8 5.4 %multiply_reduce_fusion = f32[1024,128]{1,0:T(8,128)S(1)} fusion(f32[16,1024,128]{2,1,0:T(8,128)} %bitcast.52, f32[16,1024]{1,0:T(8,128)S(1)} %get-tuple-element.49), kind=kLoop, calls=%fused_computation.10 | loop fusion | flops 4063232 | bytes 8978432 | tf_op jit(solution)/shard_map/reduce_sum | solution.py:57
  392.2 8.1 %all-reduce.4 = (f32[128]{0:T(128)S(1)}, f32[128]{0:T(128)S(1)}, f32[128]{0:T(128)S(1)}, f32[128]{0:T(128)S(1)}) all-reduce(f32[128]{0:T(128)S(1)} %get-tuple-element.8, f32[128]{0:T(128)S(1)} %get-tuple-element.6, f32[128]{0:T(128)S(1)} %get-tuple-element.7, ...), channel_id=1, replica_groups=mesh['sub_0'=4,'sub_1'=4,'sub_2'=4,'sub_3'=2,'panel'=2] {'sub_0'}, use_global_device_ids=true, to_apply=%region_33.34 | all-reduce | flops 512 | bytes 4096 | tf_op jit(solution)/shard_map/psum | solution.py:42
  400.3 8.1 %all-reduce.2 = (f32[128]{0:T(128)S(1)}, f32[128]{0:T(128)S(1)}, f32[128]{0:T(128)S(1)}, f32[128]{0:T(128)S(1)}) all-reduce(f32[128]{0:T(128)S(1)} %get-tuple-element.28, f32[128]{0:T(128)S(1)} %get-tuple-element.29, f32[128]{0:T(128)S(1)} %get-tuple-element.30, ...), channel_id=1, replica_groups=mesh['sub_0'=4,'sub_1'=4,'sub_2'=4,'sub_3'=2,'panel'=2] {'sub_1'}, use_global_device_ids=true, to_apply=%region_34.35 | all-reduce | flops 512 | bytes 4096 | tf_op jit(solution)/shard_map/psum | solution.py:42
  408.4 11.4 %all-reduce = (f32[128]{0:T(128)S(1)}, f32[128]{0:T(128)S(1)}, f32[128]{0:T(128)S(1)}, f32[128]{0:T(128)S(1)}) all-reduce(f32[128]{0:T(128)S(1)} %get-tuple-element.21, f32[128]{0:T(128)S(1)} %get-tuple-element.22, f32[128]{0:T(128)S(1)} %get-tuple-element.23, ...), channel_id=1, replica_groups=mesh['sub_0'=4,'sub_1'=4,'sub_2'=4,'sub_3'=2,'panel'=2] {'sub_2'}, use_global_device_ids=true, to_apply=%region_35.36 | all-reduce | flops 512 | bytes 4096 | tf_op jit(solution)/shard_map/psum | solution.py:42
  419.9 4.5 %all-reduce.6 = (f32[128]{0:T(128)S(1)}, f32[128]{0:T(128)S(1)}, f32[128]{0:T(128)S(1)}, f32[128]{0:T(128)S(1)}) all-reduce(f32[128]{0:T(128)S(1)} %get-tuple-element.14, f32[128]{0:T(128)S(1)} %get-tuple-element.15, f32[128]{0:T(128)S(1)} %get-tuple-element.16, ...), channel_id=1, replica_groups=mesh['sub_0'=4,'sub_1'=4,'sub_2'=4,'sub_3'=2,'panel'=2] {'sub_3'}, use_global_device_ids=true, to_apply=%region_36.37 | all-reduce | flops 512 | bytes 4096 | tf_op jit(solution)/shard_map/psum | solution.py:42
  424.9 2.8 multiply_subtract_fusion
  (87 shorter events, 65.5 us)
Async XLA Ops:
  0.6 67.0 %copy-start = (bf16[1,1792,896]{2,1,0:T(8,128)(2,1)S(1)}, bf16[1,1792,896]{2,1,0:T(8,128)(2,1)}, u32[]{:S(2)}) copy-start(bf16[1,1792,896]{2,1,0:T(8,128)(2,1)} %param.22) | copy-start | bytes 9633796
  41.9 27.0 %copy-start.16 = (f32[128]{0:T(128)}, f32[128]{0:T(128)S(1)}, u32[]{:S(2)}) copy-start(f32[128]{0:T(128)S(1)} %psum.227) | copy-start | bytes 1540
  46.7 2.4 collective-permute-start
  46.9 64.1 %copy-start.10 = (s32[1024]{0:T(1024)}, s32[1024]{0:T(1024)S(1)}, u32[]{:S(2)}) copy-start(s32[1024]{0:T(1024)S(1)} %pad_clamp_fusion) | copy-start | bytes 12292
  48.8 6.6 %collective-permute-start.1 = (bf16[384,128]{1,0:T(8,128)(2,1)}, bf16[384,128]{1,0:T(8,128)(2,1)S(1)}, u32[]{:S(2)}, u32[]{:S(2)}) collective-permute-start(bf16[384,128]{1,0:T(8,128)(2,1)} %gather_fusion.1), channel_id=1, source_target_pairs={{2,0},{4,2},{6,4},{8,6},{10,8},{12,10},{14,12},{16,14},{18,16},{20... | collective-permute-start | bytes 294920 | tf_op jit(solution)/shard_map/ppermute | solution.py:22
  90.7 7.9 %copy-start.8 = (s32[16,1024]{1,0:T(8,128)S(1)}, s32[16,1024]{1,0:T(8,128)}, u32[]{:S(2)}) copy-start(s32[16,1024]{1,0:T(8,128)} %param.24) | copy-start | bytes 196612
  94.1 12.7 %all-to-all-start.2 = ((f32[2,1024,128]{1,2,0:T(8,128)}), f32[2,1024,128]{1,2,0:T(8,128)}, u32[]{:S(2)}, u32[]{:S(2)}) async-start(f32[2,1024,128]{1,2,0:T(8,128)} %bitcast.62), calls=%async_computation.2 | async-start | bytes 2097152 | tf_op jit(solution)/shard_map/all_to_all | solution.py:37
  98.6 30.2 %copy-start.9 = (f32[16,1024]{1,0:T(8,128)S(1)}, f32[16,1024]{1,0:T(8,128)}, u32[]{:S(2)}) copy-start(f32[16,1024]{1,0:T(8,128)} %param.25) | copy-start | bytes 196612
  98.6 40.1 %copy-start.6 = (s32[16384]{0:T(1024)}, s32[16384]{0:T(1024)S(1)}, u32[]{:S(2)}) copy-start(s32[16384]{0:T(1024)S(1)} %broadcast_clamp_fusion) | copy-start | bytes 196612
  98.6 30.2 %copy-start.14 = (f32[1024]{0:T(1024)S(1)}, f32[1024]{0:T(1024)}, u32[]{:S(2)}) copy-start(f32[1024]{0:T(1024)} %param.26) | copy-start | bytes 12292
  116.3 17.3 %collective-permute-start.2 = (f32[384,128]{1,0:T(8,128)}, f32[384,128]{1,0:T(8,128)S(1)}, u32[]{:S(2)}, u32[]{:S(2)}) collective-permute-start(f32[384,128]{1,0:T(8,128)} %gather_fusion.2), channel_id=1, source_target_pairs={{0,2},{2,4},{4,6},{6,8},{8,10},{10,12},{12,14},{14,16},{16,18},{18... | collective-permute-start | bytes 589832 | tf_op jit(solution)/shard_map/ppermute | solution.py:20
  128.8 7.6 %collective-permute-start.3 = (f32[384,128]{1,0:T(8,128)}, f32[384,128]{1,0:T(8,128)S(1)}, u32[]{:S(2)}, u32[]{:S(2)}) collective-permute-start(f32[384,128]{1,0:T(8,128)} %gather_fusion.3), channel_id=1, source_target_pairs={{2,0},{4,2},{6,4},{8,6},{10,8},{12,10},{14,12},{16,14},{18,16},{20... | collective-permute-start | bytes 589832 | tf_op jit(solution)/shard_map/ppermute | solution.py:22
  194.3 5.3 %copy-start.1 = (f32[1024,128]{1,0:T(8,128)S(1)}, f32[1024,128]{1,0:T(8,128)}, u32[]{:S(2)}) copy-start(f32[1024,128]{1,0:T(8,128)} %copy.24) | copy-start | bytes 1572868
  194.3 5.4 %copy-start.4 = (f32[1024,128]{1,0:T(8,128)S(1)}, f32[1024,128]{1,0:T(8,128)}, u32[]{:S(2)}) copy-start(f32[1024,128]{1,0:T(8,128)} %param.16) | copy-start | bytes 1572868
  194.3 37.5 %copy-start.17 = (f32[128]{0:T(128)S(1)}, f32[128]{0:T(128)}, u32[]{:S(2)}) copy-start(f32[128]{0:T(128)} %copy-done.16) | copy-start | bytes 1540
  231.8 0.5 copy-start.12
  239.8 3.4 collective-permute-start.4
  241.2 6.0 %collective-permute-start.5 = (bf16[384,128]{1,0:T(8,128)(2,1)}, bf16[384,128]{1,0:T(8,128)(2,1)S(1)}, u32[]{:S(2)}, u32[]{:S(2)}) collective-permute-start(bf16[384,128]{1,0:T(8,128)(2,1)} %gather_fusion.6), channel_id=1, source_target_pairs={{2,0},{4,2},{6,4},{8,6},{10,8},{12,10},{14,12},{16,14},{18,16},{20... | collective-permute-start | bytes 294920 | tf_op jit(solution)/shard_map/ppermute | solution.py:22
  284.7 15.7 %copy-start.11 = (s32[1024]{0:T(1024)S(1)}, s32[1024]{0:T(1024)}, u32[]{:S(2)}) copy-start(s32[1024]{0:T(1024)} %copy-done.10) | copy-start | bytes 12292
  298.3 31.9 %copy-start.7 = (s32[16384]{0:T(1024)S(1)}, s32[16384]{0:T(1024)}, u32[]{:S(2)}) copy-start(s32[16384]{0:T(1024)} %copy-done.6) | copy-start | bytes 196612
  305.7 17.1 %collective-permute-start.6 = (f32[384,128]{1,0:T(8,128)}, f32[384,128]{1,0:T(8,128)S(1)}, u32[]{:S(2)}, u32[]{:S(2)}) collective-permute-start(f32[384,128]{1,0:T(8,128)} %gather_fusion.7), channel_id=1, source_target_pairs={{0,2},{2,4},{4,6},{6,8},{8,10},{10,12},{12,14},{14,16},{16,18},{18... | collective-permute-start | bytes 589832 | tf_op jit(solution)/shard_map/ppermute | solution.py:20
  319.8 8.0 %collective-permute-start.7 = (f32[384,128]{1,0:T(8,128)}, f32[384,128]{1,0:T(8,128)S(1)}, u32[]{:S(2)}, u32[]{:S(2)}) collective-permute-start(f32[384,128]{1,0:T(8,128)} %gather_fusion.8), channel_id=1, source_target_pairs={{2,0},{4,2},{6,4},{8,6},{10,8},{12,10},{14,12},{16,14},{18,16},{20... | collective-permute-start | bytes 589832 | tf_op jit(solution)/shard_map/ppermute | solution.py:22
  385.8 5.4 %copy-start.2 = (f32[1024,128]{1,0:T(8,128)S(1)}, f32[1024,128]{1,0:T(8,128)}, u32[]{:S(2)}) copy-start(f32[1024,128]{1,0:T(8,128)} %copy.32) | copy-start | bytes 1572868
  385.8 5.4 %copy-start.3 = (f32[1024,128]{1,0:T(8,128)S(1)}, f32[1024,128]{1,0:T(8,128)}, u32[]{:S(2)}) copy-start(f32[1024,128]{1,0:T(8,128)} %get-tuple-element.46) | copy-start | bytes 1572868
  385.8 5.4 %copy-start.5 = (f32[1024,128]{1,0:T(8,128)S(1)}, f32[1024,128]{1,0:T(8,128)}, u32[]{:S(2)}) copy-start(f32[1024,128]{1,0:T(8,128)} %param.16) | copy-start | bytes 1572868
  385.8 39.1 %copy-start.13 = (f32[128]{0:T(128)S(1)}, f32[128]{0:T(128)}, u32[]{:S(2)}) copy-start(f32[128]{0:T(128)} %copy-done.12) | copy-start | bytes 1540
  424.9 2.8 copy-start.15
where the time goes:
time: 429 us; the launch traced here: 428 us
  blocking collectives  171 us (40%)
  local copies, waits for them, and re-layouts  140 us (33%)
  other arithmetic  39.1 us (9%)
  waiting for transfers between devices  36 us (8%)
  starting transfers between devices  32.9 us (8%)
  matrix products  8.16 us (2%)
    gather x2, local copies, waits for them, and re-layouts, operate(): coupled = jnp.sum(present[:, :, None] * padded[neighbours], axis=0)  111 us
    psum x12, blocking collectives, one_axis_at_a_time(): return functools.reduce(lax.psum, axes, array)  103 us
    all_to_all x3, blocking collectives, sent_and_summed(): lax.all_to_all(in_blocks(array, dim, devices), axis, 0, 0, tiled=True)  50.6 us
    ppermute x4, starting transfers between devices, padded_2(): lax.ppermute(tail, axis, [(i, (i + 1) % count) for i in range(count)])  28.1 us
    ppermute x4, waiting for transfers between devices, padded_2(): lax.ppermute(head, axis, [((i + 1) % count, i) for i in range(count)])  18.1 us
    all_to_all x2, blocking collectives, precondition(): lax.all_to_all(rounded, 'panel', split_axis=0, concat_axis=1, tiled=True)  17.1 us
    reduce_sum x2, other arithmetic, operate(): coupled = jnp.sum(present[:, :, None] * padded[neighbours], axis=0)  10.7 us
    gather x4, local copies, waits for them, and re-layouts, extend(): vector[send_rows[0, 0]]  10 us
  transfers between devices with their start and end apart: 9, of which 8 were waited for; matrix products, arithmetic and copies ran while one was open for 0% of the time, Pallas kernels for 0%

commit v1 on v0

--- a/solution.py
+++ b/solution.py
@@ -63,7 +63,12 @@
     lower_panel, upper_panel = factors
     own_rows, local_sources = vector.shape
     rounded = extend(vector, send_rows).astype(jnp.bfloat16)
-    columns = lax.all_to_all(rounded, "panel", split_axis=0, concat_axis=1, tiled=True)
+    columns = jnp.concatenate(
+        lax.all_to_all(
+            jnp.stack(jnp.split(rounded, lax.axis_size("panel"), axis=0)), "panel", 0, 0
+        ),
+        axis=1,
+    )
     inner_part = sent_and_summed(
         jnp.dot(lower_panel, columns, preferred_element_type=jnp.float32), "panel", 0
     ).astype(jnp.bfloat16)

time: 429 us -> 428 us (level)
  no operation moved by 1% of the time
where the time goes in v1:
time: 428 us; the launch traced here: 426 us
  blocking collectives  168 us (39%)
  local copies, waits for them, and re-layouts  140 us (33%)
  other arithmetic  37.7 us (9%)
  waiting for transfers between devices  36.3 us (8%)
  starting transfers between devices  32.5 us (8%)
  matrix products  10.1 us (2%)
    gather x2, local copies, waits for them, and re-layouts, operate(): coupled = jnp.sum(present[:, :, None] * padded[neighbours], axis=0)  111 us
    psum x12, blocking collectives, one_axis_at_a_time(): return functools.reduce(lax.psum, axes, array)  102 us
    all_to_all x3, blocking collectives, sent_and_summed(): lax.all_to_all(in_blocks(array, dim, devices), axis, 0, 0, tiled=True)  50.5 us
    ppermute x4, starting transfers between devices, padded_2(): lax.ppermute(tail, axis, [(i, (i + 1) % count) for i in range(count)])  27.8 us
    ppermute x4, waiting for transfers between devices, padded_2(): lax.ppermute(head, axis, [((i + 1) % count, i) for i in range(count)])  18.1 us
    all_to_all x2, blocking collectives, precondition(): lax.all_to_all(jnp.stack(jnp.split(rounded, lax.axis_size('panel'), axis=...  16.4 us
    reduce_sum x2, other arithmetic, operate(): coupled = jnp.sum(present[:, :, None] * padded[neighbours], axis=0)  10.7 us
    gather x4, local copies, waits for them, and re-layouts, extend(): vector[send_rows[0, 0]]  10 us
  transfers between devices with their start and end apart: 9, of which 8 were waited for; matrix products, arithmetic and copies ran while one was open for 0% of the time, Pallas kernels for 0%

profile of v1, /device:TPU:1, one launch (start us, length us, event | category | flops | bytes accessed | tf_op | source)
XLA Modules:
  0.0 426.0 jit_solution(7439653412749846039)
XLA Ops:
  2.1 9.3 %psum.224 = f32[128]{0:T(128)S(1)} all-reduce(f32[128]{0:T(128)S(1)} %multiply_reduce_fusion.9), channel_id=1, replica_groups=mesh['sub_0'=4,'sub_1'=4,'sub_2'=4,'sub_3'=2,'panel'=2] {'sub_0'}, use_global_device_ids=true, to_apply=%region_1.0 | all-reduce | flops 128 | bytes 1024 | tf_op jit(solution)/shard_map/psum | solution.py:42
  11.4 9.0 %psum.225 = f32[128]{0:T(128)S(1)} all-reduce(f32[128]{0:T(128)S(1)} %psum.224), channel_id=1, replica_groups=mesh['sub_0'=4,'sub_1'=4,'sub_2'=4,'sub_3'=2,'panel'=2] {'sub_1'}, use_global_device_ids=true, to_apply=%region_2.0 | all-reduce | flops 128 | bytes 1024 | tf_op jit(solution)/shard_map/psum | solution.py:42
  20.4 12.9 %psum.226 = f32[128]{0:T(128)S(1)} all-reduce(f32[128]{0:T(128)S(1)} %psum.225), channel_id=1, replica_groups=mesh['sub_0'=4,'sub_1'=4,'sub_2'=4,'sub_3'=2,'panel'=2] {'sub_2'}, use_global_device_ids=true, to_apply=%region_3.0 | all-reduce | flops 128 | bytes 1024 | tf_op jit(solution)/shard_map/psum | solution.py:42
  33.3 8.6 %psum.227 = f32[128]{0:T(128)S(1)} all-reduce(f32[128]{0:T(128)S(1)} %psum.226), channel_id=1, replica_groups=mesh['sub_0'=4,'sub_1'=4,'sub_2'=4,'sub_3'=2,'panel'=2] {'sub_3'}, use_global_device_ids=true, to_apply=%region_4.0 | all-reduce | flops 128 | bytes 1024 | tf_op jit(solution)/shard_map/psum | solution.py:42
  49.2 6.3 %collective-permute-done.1 = bf16[384,128]{1,0:T(8,128)(2,1)S(1)} collective-permute-done((bf16[384,128]{1,0:T(8,128)(2,1)}, bf16[384,128]{1,0:T(8,128)(2,1)S(1)}, u32[]{:S(2)}, u32[]{:S(2)}) %collective-permute-start.1) | collective-permute-done | bytes 98336 | tf_op jit(solution)/shard_map/ppermute | solution.py:22
  56.4 8.2 %all_to_all.30 = bf16[2,896,128]{2,1,0:T(8,128)(2,1)} all-to-all(bf16[2,896,128]{2,1,0:T(8,128)(2,1)S(1)} %pad_maximum_fusion), channel_id=1, replica_groups=mesh['sub_0'=4,'sub_1'=4,'sub_2'=4,'sub_3'=2,'panel'=2] {'panel'}, dimensions={0} | all-to-all | bytes 917504 | tf_op jit(solution)/shard_map/all_to_all | solution.py:67
  68.9 19.2 %all_to_all.31 = f32[2,896,256]{1,2,0:T(8,128)} all-to-all(f32[2,896,256]{1,2,0:T(8,128)S(1)} %bitcast.58), channel_id=1, replica_groups=mesh['sub_0'=4,'sub_1'=4,'sub_2'=4,'sub_3'=2,'panel'=2] {'panel'}, dimensions={0} | all-to-all | bytes 3670016 | tf_op jit(solution)/shard_map/all_to_all | solution.py:37
  90.6 3.5 fusion.6
  94.0 4.4 %all-to-all-start.2 = ((f32[2,1024,128]{1,2,0:T(8,128)}), f32[2,1024,128]{1,2,0:T(8,128)}, u32[]{:S(2)}, u32[]{:S(2)}) async-start(f32[2,1024,128]{1,2,0:T(8,128)} %bitcast.66), calls=%async_computation.2 | async-start | bytes 2097152 | tf_op jit(solution)/shard_map/all_to_all | solution.py:37
  98.6 8.2 %all-to-all-done.2 = f32[2,1024,128]{1,2,0:T(8,128)} async-done(((f32[2,1024,128]{1,2,0:T(8,128)}), f32[2,1024,128]{1,2,0:T(8,128)}, u32[]{:S(2)}, u32[]{:S(2)}) %all-to-all-start.2) | async-done | bytes 1048608 | tf_op jit(solution)/shard_map/all_to_all | solution.py:37
  116.3 12.4 %collective-permute-start.2 = (f32[384,128]{1,0:T(8,128)}, f32[384,128]{1,0:T(8,128)S(1)}, u32[]{:S(2)}, u32[]{:S(2)}) collective-permute-start(f32[384,128]{1,0:T(8,128)} %gather_fusion.2), channel_id=1, source_target_pairs={{0,2},{2,4},{4,6},{6,8},{8,10},{10,12},{12,14},{14,16},{16,18},{18... | collective-permute-start | bytes 589832 | tf_op jit(solution)/shard_map/ppermute | solution.py:20
  128.7 5.0 %collective-permute-done.2 = f32[384,128]{1,0:T(8,128)S(1)} collective-permute-done((f32[384,128]{1,0:T(8,128)}, f32[384,128]{1,0:T(8,128)S(1)}, u32[]{:S(2)}, u32[]{:S(2)}) %collective-permute-start.2) | collective-permute-done | bytes 196640 | tf_op jit(solution)/shard_map/ppermute | solution.py:20
  138.6 55.6 %gather_fusion.4 = f32[16384,128]{1,0:T(8,128)} fusion(f32[1793,128]{1,0:T(8,128)} %maximum_maximum_fusion, s32[16384]{0:T(1024)S(1)} %broadcast_clamp_fusion), kind=kCustom, calls=%fused_computation.4 | custom fusion | bytes 16842752 | tf_op jit(solution)/shard_map/gather | solution.py:57
  194.2 5.3 %multiply_reduce_fusion.1 = f32[1024,128]{1,0:T(8,128)S(1)} fusion(f32[16,1024,128]{2,1,0:T(8,128)} %bitcast.57, f32[16,1024]{1,0:T(8,128)S(1)} %get-tuple-element.49), kind=kLoop, calls=%fused_computation.11 | loop fusion | flops 4063232 | bytes 8978432 | tf_op jit(solution)/shard_map/reduce_sum | solution.py:57
  200.6 6.2 %all-reduce.5 = (f32[128]{0:T(128)S(1)}, f32[128]{0:T(128)S(1)}, f32[128]{0:T(128)S(1)}) all-reduce(f32[128]{0:T(128)S(1)} %get-tuple-element.10, f32[128]{0:T(128)S(1)} %get-tuple-element.11, f32[128]{0:T(128)S(1)} %get-tuple-element.9), channel_id=1, replica_groups=mesh['sub_0'=4,'sub_1'=4,'sub_2'=4,'sub_3'=2,'panel'=2] {'sub_0'}, use_global_device_ids=true, to_apply=%region_20.21 | all-reduce | flops 384 | bytes 3072 | tf_op jit(solution)/shard_map/psum | solution.py:42
  206.8 6.0 %all-reduce.3 = (f32[128]{0:T(128)S(1)}, f32[128]{0:T(128)S(1)}, f32[128]{0:T(128)S(1)}) all-reduce(f32[128]{0:T(128)S(1)} %get-tuple-element.32, f32[128]{0:T(128)S(1)} %get-tuple-element.33, f32[128]{0:T(128)S(1)} %get-tuple-element.34), channel_id=1, replica_groups=mesh['sub_0'=4,'sub_1'=4,'sub_2'=4,'sub_3'=2,'panel'=2] {'sub_1'}, use_global_device_ids=true, to_apply=%region_21.22 | all-reduce | flops 384 | bytes 3072 | tf_op jit(solution)/shard_map/psum | solution.py:42
  212.8 16.4 %all-reduce.1 = (f32[128]{0:T(128)S(1)}, f32[128]{0:T(128)S(1)}, f32[128]{0:T(128)S(1)}) all-reduce(f32[128]{0:T(128)S(1)} %get-tuple-element.25, f32[128]{0:T(128)S(1)} %get-tuple-element.26, f32[128]{0:T(128)S(1)} %get-tuple-element.27), channel_id=1, replica_groups=mesh['sub_0'=4,'sub_1'=4,'sub_2'=4,'sub_3'=2,'panel'=2] {'sub_2'}, use_global_device_ids=true, to_apply=%region_22.23 | all-reduce | flops 384 | bytes 3072 | tf_op jit(solution)/shard_map/psum | solution.py:42
  234.2 2.8 gather_fusion.6
  242.8 4.2 collective-permute-done.5
  247.1 8.2 %all_to_all.32 = bf16[2,896,128]{2,1,0:T(8,128)(2,1)} all-to-all(bf16[2,896,128]{2,1,0:T(8,128)(2,1)S(1)} %pad_maximum_fusion.1), channel_id=1, replica_groups=mesh['sub_0'=4,'sub_1'=4,'sub_2'=4,'sub_3'=2,'panel'=2] {'panel'}, dimensions={0} | all-to-all | bytes 917504 | tf_op jit(solution)/shard_map/all_to_all | solution.py:67
  259.6 19.9 %all_to_all.33 = f32[2,896,256]{1,2,0:T(8,128)} all-to-all(f32[2,896,256]{1,2,0:T(8,128)S(1)} %bitcast.59), channel_id=1, replica_groups=mesh['sub_0'=4,'sub_1'=4,'sub_2'=4,'sub_3'=2,'panel'=2] {'panel'}, dimensions={0} | all-to-all | bytes 3670016 | tf_op jit(solution)/shard_map/all_to_all | solution.py:37
  284.4 11.5 %all_to_all.34 = f32[2,1024,128]{1,2,0:T(8,128)} all-to-all(f32[2,1024,128]{1,2,0:T(8,128)S(1)} %bitcast.67), channel_id=1, replica_groups=mesh['sub_0'=4,'sub_1'=4,'sub_2'=4,'sub_3'=2,'panel'=2] {'panel'}, dimensions={0} | all-to-all | bytes 2097152 | tf_op jit(solution)/shard_map/all_to_all | solution.py:37
  305.4 14.1 %collective-permute-start.6 = (f32[384,128]{1,0:T(8,128)}, f32[384,128]{1,0:T(8,128)S(1)}, u32[]{:S(2)}, u32[]{:S(2)}) collective-permute-start(f32[384,128]{1,0:T(8,128)} %gather_fusion.7), channel_id=1, source_target_pairs={{0,2},{2,4},{4,6},{6,8},{8,10},{10,12},{12,14},{14,16},{16,18},{18... | collective-permute-start | bytes 589832 | tf_op jit(solution)/shard_map/ppermute | solution.py:20
  319.5 3.0 collective-permute-done.6
  322.5 5.1 %collective-permute-done.7 = f32[384,128]{1,0:T(8,128)S(1)} collective-permute-done((f32[384,128]{1,0:T(8,128)}, f32[384,128]{1,0:T(8,128)S(1)}, u32[]{:S(2)}, u32[]{:S(2)}) %collective-permute-start.7) | collective-permute-done | bytes 196640 | tf_op jit(solution)/shard_map/ppermute | solution.py:22
  329.9 55.6 %gather_fusion.9 = f32[16384,128]{1,0:T(8,128)} fusion(f32[1793,128]{1,0:T(8,128)} %maximum_maximum_fusion.1, s32[16384]{0:T(1024)S(1)} %copy-done.7), kind=kCustom, calls=%fused_computation.9 | custom fusion | bytes 16842752 | tf_op jit(solution)/shard_map/gather | solution.py:57
  385.5 5.4 %multiply_reduce_fusion = f32[1024,128]{1,0:T(8,128)S(1)} fusion(f32[16,1024,128]{2,1,0:T(8,128)} %bitcast.56, f32[16,1024]{1,0:T(8,128)S(1)} %get-tuple-element.49), kind=kLoop, calls=%fused_computation.10 | loop fusion | flops 4063232 | bytes 8978432 | tf_op jit(solution)/shard_map/reduce_sum | solution.py:57
  391.9 8.2 %all-reduce.4 = (f32[128]{0:T(128)S(1)}, f32[128]{0:T(128)S(1)}, f32[128]{0:T(128)S(1)}, f32[128]{0:T(128)S(1)}) all-reduce(f32[128]{0:T(128)S(1)} %get-tuple-element.8, f32[128]{0:T(128)S(1)} %get-tuple-element.6, f32[128]{0:T(128)S(1)} %get-tuple-element.7, ...), channel_id=1, replica_groups=mesh['sub_0'=4,'sub_1'=4,'sub_2'=4,'sub_3'=2,'panel'=2] {'sub_0'}, use_global_device_ids=true, to_apply=%region_33.34 | all-reduce | flops 512 | bytes 4096 | tf_op jit(solution)/shard_map/psum | solution.py:42
  400.1 6.0 %all-reduce.2 = (f32[128]{0:T(128)S(1)}, f32[128]{0:T(128)S(1)}, f32[128]{0:T(128)S(1)}, f32[128]{0:T(128)S(1)}) all-reduce(f32[128]{0:T(128)S(1)} %get-tuple-element.28, f32[128]{0:T(128)S(1)} %get-tuple-element.29, f32[128]{0:T(128)S(1)} %get-tuple-element.30, ...), channel_id=1, replica_groups=mesh['sub_0'=4,'sub_1'=4,'sub_2'=4,'sub_3'=2,'panel'=2] {'sub_1'}, use_global_device_ids=true, to_apply=%region_34.35 | all-reduce | flops 512 | bytes 4096 | tf_op jit(solution)/shard_map/psum | solution.py:42
  406.1 12.3 %all-reduce = (f32[128]{0:T(128)S(1)}, f32[128]{0:T(128)S(1)}, f32[128]{0:T(128)S(1)}, f32[128]{0:T(128)S(1)}) all-reduce(f32[128]{0:T(128)S(1)} %get-tuple-element.21, f32[128]{0:T(128)S(1)} %get-tuple-element.22, f32[128]{0:T(128)S(1)} %get-tuple-element.23, ...), channel_id=1, replica_groups=mesh['sub_0'=4,'sub_1'=4,'sub_2'=4,'sub_3'=2,'panel'=2] {'sub_2'}, use_global_device_ids=true, to_apply=%region_35.36 | all-reduce | flops 512 | bytes 4096 | tf_op jit(solution)/shard_map/psum | solution.py:42
  418.4 4.3 %all-reduce.6 = (f32[128]{0:T(128)S(1)}, f32[128]{0:T(128)S(1)}, f32[128]{0:T(128)S(1)}, f32[128]{0:T(128)S(1)}) all-reduce(f32[128]{0:T(128)S(1)} %get-tuple-element.14, f32[128]{0:T(128)S(1)} %get-tuple-element.15, f32[128]{0:T(128)S(1)} %get-tuple-element.16, ...), channel_id=1, replica_groups=mesh['sub_0'=4,'sub_1'=4,'sub_2'=4,'sub_3'=2,'panel'=2] {'sub_3'}, use_global_device_ids=true, to_apply=%region_36.37 | all-reduce | flops 512 | bytes 4096 | tf_op jit(solution)/shard_map/psum | solution.py:42
  423.2 2.8 multiply_subtract_fusion
  (89 shorter events, 65.5 us)
Async XLA Ops:
  0.6 66.0 %copy-start = (bf16[1,1792,896]{2,1,0:T(8,128)(2,1)S(1)}, bf16[1,1792,896]{2,1,0:T(8,128)(2,1)}, u32[]{:S(2)}) copy-start(bf16[1,1792,896]{2,1,0:T(8,128)(2,1)} %param.22) | copy-start | bytes 9633796
  41.9 22.7 %copy-start.16 = (f32[128]{0:T(128)}, f32[128]{0:T(128)S(1)}, u32[]{:S(2)}) copy-start(f32[128]{0:T(128)S(1)} %psum.227) | copy-start | bytes 1540
  46.7 2.4 collective-permute-start
  46.9 64.0 %copy-start.10 = (s32[1024]{0:T(1024)}, s32[1024]{0:T(1024)S(1)}, u32[]{:S(2)}) copy-start(s32[1024]{0:T(1024)S(1)} %pad_clamp_fusion) | copy-start | bytes 12292
  48.8 6.6 %collective-permute-start.1 = (bf16[384,128]{1,0:T(8,128)(2,1)}, bf16[384,128]{1,0:T(8,128)(2,1)S(1)}, u32[]{:S(2)}, u32[]{:S(2)}) collective-permute-start(bf16[384,128]{1,0:T(8,128)(2,1)} %gather_fusion.1), channel_id=1, source_target_pairs={{2,0},{4,2},{6,4},{8,6},{10,8},{12,10},{14,12},{16,14},{18,16},{20... | collective-permute-start | bytes 294920 | tf_op jit(solution)/shard_map/ppermute | solution.py:22
  90.6 7.9 %copy-start.8 = (s32[16,1024]{1,0:T(8,128)S(1)}, s32[16,1024]{1,0:T(8,128)}, u32[]{:S(2)}) copy-start(s32[16,1024]{1,0:T(8,128)} %param.24) | copy-start | bytes 196612
  94.0 12.7 %all-to-all-start.2 = ((f32[2,1024,128]{1,2,0:T(8,128)}), f32[2,1024,128]{1,2,0:T(8,128)}, u32[]{:S(2)}, u32[]{:S(2)}) async-start(f32[2,1024,128]{1,2,0:T(8,128)} %bitcast.66), calls=%async_computation.2 | async-start | bytes 2097152 | tf_op jit(solution)/shard_map/all_to_all | solution.py:37
  98.5 30.2 %copy-start.9 = (f32[16,1024]{1,0:T(8,128)S(1)}, f32[16,1024]{1,0:T(8,128)}, u32[]{:S(2)}) copy-start(f32[16,1024]{1,0:T(8,128)} %param.25) | copy-start | bytes 196612
  98.5 40.1 %copy-start.6 = (s32[16384]{0:T(1024)}, s32[16384]{0:T(1024)S(1)}, u32[]{:S(2)}) copy-start(s32[16384]{0:T(1024)S(1)} %broadcast_clamp_fusion) | copy-start | bytes 196612
  98.6 30.2 %copy-start.14 = (f32[1024]{0:T(1024)S(1)}, f32[1024]{0:T(1024)}, u32[]{:S(2)}) copy-start(f32[1024]{0:T(1024)} %param.26) | copy-start | bytes 12292
  116.3 17.5 %collective-permute-start.2 = (f32[384,128]{1,0:T(8,128)}, f32[384,128]{1,0:T(8,128)S(1)}, u32[]{:S(2)}, u32[]{:S(2)}) collective-permute-start(f32[384,128]{1,0:T(8,128)} %gather_fusion.2), channel_id=1, source_target_pairs={{0,2},{2,4},{4,6},{6,8},{8,10},{10,12},{12,14},{14,16},{16,18},{18... | collective-permute-start | bytes 589832 | tf_op jit(solution)/shard_map/ppermute | solution.py:20
  128.7 7.6 %collective-permute-start.3 = (f32[384,128]{1,0:T(8,128)}, f32[384,128]{1,0:T(8,128)S(1)}, u32[]{:S(2)}, u32[]{:S(2)}) collective-permute-start(f32[384,128]{1,0:T(8,128)} %gather_fusion.3), channel_id=1, source_target_pairs={{2,0},{4,2},{6,4},{8,6},{10,8},{12,10},{14,12},{16,14},{18,16},{20... | collective-permute-start | bytes 589832 | tf_op jit(solution)/shard_map/ppermute | solution.py:22
  194.2 5.3 %copy-start.1 = (f32[1024,128]{1,0:T(8,128)S(1)}, f32[1024,128]{1,0:T(8,128)}, u32[]{:S(2)}) copy-start(f32[1024,128]{1,0:T(8,128)} %copy.24) | copy-start | bytes 1572868
  194.2 5.4 %copy-start.4 = (f32[1024,128]{1,0:T(8,128)S(1)}, f32[1024,128]{1,0:T(8,128)}, u32[]{:S(2)}) copy-start(f32[1024,128]{1,0:T(8,128)} %param.16) | copy-start | bytes 1572868
  194.2 37.4 %copy-start.17 = (f32[128]{0:T(128)S(1)}, f32[128]{0:T(128)}, u32[]{:S(2)}) copy-start(f32[128]{0:T(128)} %copy-done.16) | copy-start | bytes 1540
  231.6 0.5 copy-start.12
  239.7 3.1 collective-permute-start.4
  240.8 6.2 %collective-permute-start.5 = (bf16[384,128]{1,0:T(8,128)(2,1)}, bf16[384,128]{1,0:T(8,128)(2,1)S(1)}, u32[]{:S(2)}, u32[]{:S(2)}) collective-permute-start(bf16[384,128]{1,0:T(8,128)(2,1)} %gather_fusion.6), channel_id=1, source_target_pairs={{2,0},{4,2},{6,4},{8,6},{10,8},{12,10},{14,12},{16,14},{18,16},{20... | collective-permute-start | bytes 294920 | tf_op jit(solution)/shard_map/ppermute | solution.py:22
  284.4 15.7 %copy-start.11 = (s32[1024]{0:T(1024)S(1)}, s32[1024]{0:T(1024)}, u32[]{:S(2)}) copy-start(s32[1024]{0:T(1024)} %copy-done.10) | copy-start | bytes 12292
  298.0 31.9 %copy-start.7 = (s32[16384]{0:T(1024)S(1)}, s32[16384]{0:T(1024)}, u32[]{:S(2)}) copy-start(s32[16384]{0:T(1024)} %copy-done.6) | copy-start | bytes 196612
  305.4 17.1 %collective-permute-start.6 = (f32[384,128]{1,0:T(8,128)}, f32[384,128]{1,0:T(8,128)S(1)}, u32[]{:S(2)}, u32[]{:S(2)}) collective-permute-start(f32[384,128]{1,0:T(8,128)} %gather_fusion.7), channel_id=1, source_target_pairs={{0,2},{2,4},{4,6},{6,8},{8,10},{10,12},{12,14},{14,16},{16,18},{18... | collective-permute-start | bytes 589832 | tf_op jit(solution)/shard_map/ppermute | solution.py:20
  319.5 8.0 %collective-permute-start.7 = (f32[384,128]{1,0:T(8,128)}, f32[384,128]{1,0:T(8,128)S(1)}, u32[]{:S(2)}, u32[]{:S(2)}) collective-permute-start(f32[384,128]{1,0:T(8,128)} %gather_fusion.8), channel_id=1, source_target_pairs={{2,0},{4,2},{6,4},{8,6},{10,8},{12,10},{14,12},{16,14},{18,16},{20... | collective-permute-start | bytes 589832 | tf_op jit(solution)/shard_map/ppermute | solution.py:22
  385.5 5.4 %copy-start.2 = (f32[1024,128]{1,0:T(8,128)S(1)}, f32[1024,128]{1,0:T(8,128)}, u32[]{:S(2)}) copy-start(f32[1024,128]{1,0:T(8,128)} %copy.32) | copy-start | bytes 1572868
  385.5 5.4 %copy-start.3 = (f32[1024,128]{1,0:T(8,128)S(1)}, f32[1024,128]{1,0:T(8,128)}, u32[]{:S(2)}) copy-start(f32[1024,128]{1,0:T(8,128)} %get-tuple-element.46) | copy-start | bytes 1572868
  385.5 5.4 %copy-start.5 = (f32[1024,128]{1,0:T(8,128)S(1)}, f32[1024,128]{1,0:T(8,128)}, u32[]{:S(2)}) copy-start(f32[1024,128]{1,0:T(8,128)} %param.16) | copy-start | bytes 1572868
  385.5 37.8 %copy-start.13 = (f32[128]{0:T(128)S(1)}, f32[128]{0:T(128)}, u32[]{:S(2)}) copy-start(f32[128]{0:T(128)} %copy-done.12) | copy-start | bytes 1540
  423.2 2.8 copy-start.15
